TPU v7x, 32 devices: a whole 2x2x4 slice. The times are simulated.
32 devices in a mesh: dom: 8 (over z, y), case: 4 (over x, core).
Axes of the slice: x: 2, y: 2, z: 4, core: 2. Of those that a mesh axis runs over, the one named last changes fastest.
Arguments:
- dual_ops: float32 [16, 1536, 1536], P('dom')
- modes: bfloat16 [16, 16, 1536], P('dom'), may hold values from -0.15625 to 0.15625
- coarse_rows: float32 [16, 8, 16, 16], P('dom'), may hold values from -1 to 1
- coarse_cols: int32 [16, 8], P('dom'), may hold values from 0 to 15, as said below
- row_perm: int32 [16, 1536], P('dom'), may hold values from 0 to 1535, each once within a row
- iface_size: int32 [16], P('dom'), may hold values from 256 to 768, as said below
- rhs: float32 [16, 768, 512], P('dom', None, 'case'), may hold values from -6 to 6
Outputs:
- solution: float32 [16, 768, 512], P('dom', None, 'case')
- residual: float32 [16, 768, 512], P('dom', None, 'case')
- history: float32 [4, 512], P(None, 'case')
- peak_norm: float32 [4], replicated
Inputs may be any that keep to these rules, and one draw needn't show every extreme that they name: `iface_size`: interfaces carry between 256 and 768 multipliers; both ends are reached in every draw. `coarse_cols`: for every subdomain s the first three entries are s, (s - 1) mod 16 and (s + 1) mod 16; the others are any subdomains, repeats allowed. `row_perm`: each row is a permutation of the local rows.
All inputs are finite; a program needn't handle non-finite values.
Results may differ from a plain program's by a relative error of at most 0.0056.
Values may be sent and summed in bfloat16 or wider, within the bound.
A program may use at most 192 MiB of HBM per device.

v0:
```python
import jax
import jax.numpy as jnp
from jax import lax
from jax.sharding import PartitionSpec as P

STEPS = 4
low_bound = 2.0
high_bound = 14.0
epsilon = 1e-06
highest = lax.Precision.HIGHEST


def from_behind(block, axis, distance):
    devices = range(lax.axis_size(axis))
    route = [((i - distance) % len(devices), i) for i in devices]
    return lax.ppermute(block, axis, route)


def slot_form(left_side, right_side):
    return jnp.concatenate([-left_side, right_side], axis=1)


def shards(dual_ops, modes, coarse_rows, coarse_cols, row_perm, iface_size, rhs):
    sub_count, half_width, case_count = rhs.shape
    dom_count = lax.axis_size("dom") * sub_count
    live_mask = (
        lax.broadcasted_iota(jnp.int32, (sub_count, half_width), 1) < iface_size[:, None]
    ).astype(jnp.float32)[:, :, None]
    slot_ops = jax.vmap(lambda matrix, ordering: matrix[ordering].T[ordering])(dual_ops, row_perm)
    slot_modes_low = jax.vmap(lambda block_rows, ordering: block_rows[:, ordering])(modes, row_perm)
    slot_modes = slot_modes_low.astype(jnp.float32)
    int_pack = jnp.concatenate([coarse_cols, iface_size[:, None]], axis=1)
    prior_ints = from_behind(int_pack[-1], "dom", 1)
    next_ints = from_behind(int_pack[0], "dom", -1)
    prior_modes = from_behind(slot_modes_low[-1], "dom", 1)
    next_modes = from_behind(slot_modes_low[0], "dom", -1)
    prior_blocks = from_behind(coarse_rows[-1], "dom", 1)
    next_blocks = from_behind(coarse_rows[0], "dom", -1)
    ext_ints = jnp.concatenate([prior_ints[None], int_pack, next_ints[None]], axis=0)
    block_count = coarse_cols.shape[1]
    ext_cols = ext_ints[:, :block_count]
    ext_size = ext_ints[:, block_count]
    ext_modes = jnp.concatenate(
        [prior_modes[None], slot_modes_low, next_modes[None]], axis=0
    ).astype(jnp.float32)
    ext_blocks = jnp.concatenate([prior_blocks[None], coarse_rows, next_blocks[None]], axis=0)
    ext_live = (
        lax.broadcasted_iota(jnp.int32, (sub_count + 2, half_width), 1) < ext_size[:, None]
    ).astype(jnp.float32)[:, :, None]

    def build_local(vector):
        prior_rim = from_behind(vector[-1], "dom", 1)
        left_side = jnp.concatenate([prior_rim[None], vector[:-1]], axis=0)
        return slot_form(left_side, vector)

    def select_columns(columns, all_coefficients):
        table = (
            columns[:, :, None] == lax.broadcasted_iota(jnp.int32, (1, 1, dom_count), 2)
        ).astype(jnp.float32)
        return jnp.einsum(
            "sqd,djc->sqjc", table, all_coefficients.astype(jnp.float32), precision=highest
        )

    def gather_coefficients(slot_rows):
        coefficients = jnp.einsum("sjn,snc->sjc", slot_modes, slot_rows, precision=highest).astype(
            jnp.bfloat16
        )
        return lax.all_gather(coefficients, "dom", axis=0, tiled=True)

    centre = 0.5 * (high_bound + low_bound)
    radius = 0.5 * (high_bound - low_bound)
    spread_ratio = centre / radius
    ratio_now = 1.0 / spread_ratio
    start_vector = rhs * live_mask
    picked = select_columns(coarse_cols, gather_coefficients(build_local(start_vector)))
    amounts = jnp.einsum("sqij,sqjc->sic", coarse_rows, picked, precision=highest)
    slot_rows = jnp.einsum("sjn,sjc->snc", slot_modes, amounts, precision=highest)
    lower_half = slot_rows[:, :half_width]
    upper_half = slot_rows[:, half_width:]
    later_rim = from_behind(lower_half[0], "dom", -1)
    following = jnp.concatenate([lower_half[1:], later_rim[None]], axis=0)
    residual = start_vector - (upper_half - following) * live_mask
    direction = residual / centre
    local_residual = build_local(residual)
    local_direction = local_residual / centre
    solution = jnp.zeros_like(rhs)
    norm_list = []
    for turn_index in range(STEPS):
        solution = solution + direction
        product = jnp.einsum("smn,smc->snc", slot_ops, local_direction, precision=highest)
        local_lower_half = product[:, :half_width]
        local_upper_half = product[:, half_width:]
        prior_upper = from_behind(local_upper_half[-1], "dom", 1)
        later_lower = from_behind(local_lower_half[0], "dom", -1)
        local_following = jnp.concatenate([local_lower_half[1:], later_lower[None]], axis=0)
        mapped = (local_upper_half - local_following) * live_mask
        first_value = (prior_upper - local_lower_half[0]) * ext_live[0]
        local_left_side = jnp.concatenate([first_value[None], mapped[:-1]], axis=0)
        mapped, local_mapped = (mapped, slot_form(local_left_side, mapped))
        wide_picked = select_columns(ext_cols, gather_coefficients(local_mapped))
        wide_amounts = jnp.einsum("sqij,sqjc->sic", ext_blocks, wide_picked, precision=highest)
        spread = jnp.einsum("sjn,sjc->snc", ext_modes, wide_amounts, precision=highest)
        lower_part = spread[:, :half_width]
        upper_part = spread[:, half_width:]
        joined = (upper_part[:-1] - lower_part[1:]) * ext_live[:-1]
        correction = joined[1:]
        local_correction = slot_form(joined[:-1], joined[1:])
        residual = residual - (mapped - correction)
        local_residual = local_residual - (local_mapped - local_correction)
        partial_value = jnp.sum(residual * residual, axis=(0, 1))
        norm_list.append(jnp.sqrt(lax.psum(partial_value, "dom") + epsilon))
        if turn_index + 1 < STEPS:
            ratio_next = 1.0 / (2.0 * spread_ratio - ratio_now)
            direction = ratio_next * ratio_now * direction + 2.0 * ratio_next / radius * residual
            local_direction = (
                ratio_next * ratio_now * local_direction
                + 2.0 * ratio_next / radius * local_residual
            )
            ratio_now = ratio_next
    history = jnp.stack(norm_list)
    peak_norm = lax.pmax(jnp.max(history, axis=1), "case")
    return (solution, residual, history, peak_norm)


def solution(mesh):
    in_specs = (
        P("dom", None, None),
        P("dom", None, None),
        P("dom", None, None, None),
        P("dom", None),
        P("dom", None),
        P("dom"),
        P("dom", None, "case"),
    )
    out_specs = (P("dom", None, "case"), P("dom", None, "case"), P(None, "case"), P())
    return jax.shard_map(shards, mesh=mesh, in_specs=in_specs, out_specs=out_specs, check_vma=False)
```

profile of v0, /device:TPU:0, one launch (start us, length us, event | category | flops | bytes accessed | tf_op | source)
XLA Modules:
  0.0 592.4 jit_solution(7699816429259120163)
XLA Ops:
  7.3 16.5 %gather_fusion = bf16[3072,16]{1,0:T(8,128)(2,1)S(1)} fusion(bf16[2,16,1536]{1,2,0:T(8,128)(2,1)S(1)} %copy.28, s32[3072]{0:T(1024)S(1)} %reshape.35), kind=kCustom, calls=%fused_computation | custom fusion | bytes 221184 | tf_op jit(solution)/shard_map/vmap()/gather | solution.py:30
  24.8 30.9 %all_gather.15 = bf16[16,16,128]{2,1,0:T(8,128)(2,1)S(1)} all-gather(bf16[2,16,128]{2,1,0:T(8,128)(2,1)S(1)} %fusion.33), channel_id=1, replica_groups=mesh['dom'=8,'case'=4] {'dom'}, dimensions={0}, use_global_device_ids=true | all-gather | bytes 73728 | tf_op jit(solution)/shard_map/all_gather | solution.py:68
  66.2 68.1 %gather_fusion.1 = f32[3072,1536]{1,0:T(8,128)} fusion(f32[2,1536,1536]{2,1,0:T(8,128)} %param.7, s32[3072]{0:T(1024)S(1)} %reshape.35), kind=kCustom, calls=%fused_computation.1 | custom fusion | bytes 37773312 | tf_op jit(solution)/shard_map/vmap()/gather | solution.py:29
  134.3 18.7 %copy.34 = f32[2,1536,1536]{1,2,0:T(8,128)} copy(f32[2,1536,1536]{2,1,0:T(8,128)} %bitcast.153) | data formatting | bytes 37748736 | tf_op jit(solution)/shard_map/vmap()/gather | solution.py:29
  153.0 68.1 %gather_fusion.2 = f32[3072,1536]{1,0:T(8,128)} fusion(f32[2,1536,1536]{2,1,0:T(8,128)} %bitcast.146, s32[3072]{0:T(1024)S(1)} %reshape.35), kind=kCustom, calls=%fused_computation.2 | custom fusion | bytes 37773312 | tf_op jit(solution)/shard_map/vmap()/gather | solution.py:29
  224.0 4.5 collective-permute-start.5
  228.6 5.4 collective-permute-done.2
  234.1 32.9 %fusion.18 = f32[2,1536,128]{2,1,0:T(8,128)S(1)} fusion(f32[2,1536,1536]{2,1,0:T(8,128)} %bitcast.147, f32[2,768,128]{2,1,0:T(8,128)S(1)} %fusion.44, f32[2,768,128]{2,1,0:T(8,128)S(1)} %maximum_negate_fusion.1), kind=kOutput, calls=%fused_computation.29 | convolution fusion | flops 7248543744 | bytes 22020096 | tf_op jit(solution)/shard_map/smn,smc->snc/dot_general | solution.py:90
  270.1 5.5 collective-permute-done.3
  275.9 4.6 collective-permute-done.10
  281.7 30.7 %all_gather.16 = bf16[16,16,128]{2,1,0:T(8,128)(2,1)S(1)} all-gather(bf16[2,16,128]{2,1,0:T(8,128)(2,1)S(1)} %fusion.27), channel_id=1, replica_groups=mesh['dom'=8,'case'=4] {'dom'}, dimensions={0}, use_global_device_ids=true | all-gather | bytes 73728 | tf_op jit(solution)/shard_map/all_gather | solution.py:68
  317.5 31.7 %fusion.115 = f32[2,1536,128]{2,1,0:T(8,128)S(1)} fusion(f32[2,1536,1536]{2,1,0:T(8,128)S(1)} %bitcast.150, f32[2,1536,128]{2,1,0:T(8,128)S(1)} %multiply_add_fusion.1), kind=kOutput, calls=%fused_computation.185 | convolution fusion | flops 7247757312 | bytes 22020096 | tf_op jit(solution)/shard_map/smn,smc->snc/dot_general | solution.py:90
  351.3 5.8 collective-permute-done.11
  362.7 30.5 %all_gather.17 = bf16[16,16,128]{2,1,0:T(8,128)(2,1)S(1)} all-gather(bf16[2,16,128]{2,1,0:T(8,128)(2,1)S(1)} %fusion.28), channel_id=1, replica_groups=mesh['dom'=8,'case'=4] {'dom'}, dimensions={0}, use_global_device_ids=true | all-gather | bytes 73728 | tf_op jit(solution)/shard_map/all_gather | solution.py:68
  399.7 33.1 %fusion.20 = f32[2,1536,128]{2,1,0:T(8,128)} fusion(f32[2,1536,1536]{2,1,0:T(8,128)S(1)} %bitcast.151, f32[2,1536,128]{2,1,0:T(8,128)} %fusion.5, f32[2,1536,128]{2,1,0:T(8,128)S(1)} %multiply_add_fusion.1), kind=kOutput, calls=%fused_computation.31 | convolution fusion | flops 7248936960 | bytes 23592960 | tf_op jit(solution)/shard_map/smn,smc->snc/dot_general | solution.py:90
  436.3 5.8 collective-permute-done.13
  442.6 4.3 collective-permute-done.14
  448.1 30.5 %all_gather.18 = bf16[16,16,128]{2,1,0:T(8,128)(2,1)S(1)} all-gather(bf16[2,16,128]{2,1,0:T(8,128)(2,1)S(1)} %fusion.29), channel_id=1, replica_groups=mesh['dom'=8,'case'=4] {'dom'}, dimensions={0}, use_global_device_ids=true | all-gather | bytes 73728 | tf_op jit(solution)/shard_map/all_gather | solution.py:68
  484.1 32.5 %fusion.9 = f32[2,1536,128]{2,1,0:T(8,128)S(1)} fusion(f32[2,1536,1536]{2,1,0:T(8,128)S(1)} %bitcast.152, f32[2,1536,128]{2,1,0:T(8,128)S(1)} %copy-done, f32[2,768,128]{2,1,0:T(8,128)} %get-tuple-element.35, f32[2,768,128]{2,1,0:T(8,128)} %get-tuple-element.34, f32[2,1536,128]{2,1,0:T(8,128)S(1)} %multiply_add_fusion.1, f32[2,768,128]{2,1,0:T(8,128)S(1)} %fusion.40, ...), kind=kOutput, calls=%fused_computation.19 | convolution fusion | flops 7251689472 | bytes 26738688 | tf_op jit(solution)/shard_map/smn,smc->snc/dot_general | solution.py:90
  518.8 5.8 collective-permute-done.15
  525.0 4.0 collective-permute-done.16
  530.2 30.5 %all_gather.19 = bf16[16,16,128]{2,1,0:T(8,128)(2,1)S(1)} all-gather(bf16[2,16,128]{2,1,0:T(8,128)(2,1)S(1)} %fusion.30), channel_id=1, replica_groups=mesh['dom'=8,'case'=4] {'dom'}, dimensions={0}, use_global_device_ids=true | all-gather | bytes 73728 | tf_op jit(solution)/shard_map/all_gather | solution.py:68
  566.3 19.1 %all-reduce = (f32[128]{0:T(128)S(1)}, f32[128]{0:T(128)S(1)}, f32[128]{0:T(128)S(1)}, f32[128]{0:T(128)S(1)}) all-reduce(f32[128]{0:T(128)S(1)} %get-tuple-element.16, f32[128]{0:T(128)S(1)} %get-tuple-element.14, f32[128]{0:T(128)S(1)} %get-tuple-element.12, f32[128]{0:T(128)S(1)} %get-tuple-element.10), channel_id=1, replica_groups=mesh['dom'=8,'case'=4] {'dom'}, use_global_device_ids=true, to_apply=%region_7.0 | all-reduce | flops 512 | bytes 4096 | tf_op jit(solution)/shard_map/psum | solution.py:111
  586.0 6.2 %pmax.7 = f32[4]{0:T(128)} all-reduce(f32[4]{0:T(128)S(1)} %get-tuple-element.8), channel_id=1, replica_groups=mesh['dom'=8,'case'=4] {'case'}, use_global_device_ids=true, to_apply=%region_9.0 | all-reduce | flops 4 | bytes 32 | tf_op jit(solution)/shard_map/pmax | solution.py:121
  (142 shorter events, 65.3 us)
Async XLA Ops:
  3.6 20.2 %collective-permute-start = (f32[768,128]{1,0:T(8,128)}, f32[768,128]{1,0:T(8,128)S(1)}, u32[]{:S(2)}, u32[]{:S(2)}) collective-permute-start(f32[768,128]{1,0:T(8,128)} %get-tuple-element.43), channel_id=1, source_target_pairs={{28,0},{0,4},{4,8},{8,12},{12,16},{16,20},{20,24},{24,28},{29,1},{... | collective-permute-start | bytes 1179656 | tf_op jit(solution)/shard_map/ppermute | solution.py:16
  7.0 16.8 %copy-start.13 = (s32[2,8]{1,0:T(2,128)S(1)}, s32[2,8]{1,0:T(2,128)}, u32[]{:S(2)}) copy-start(s32[2,8]{1,0:T(2,128)} %param.10) | copy-start | bytes 196
  57.9 163.1 %collective-permute-start.1 = (f32[768,128]{1,0:T(8,128)S(1)}, f32[768,128]{1,0:T(8,128)S(1)}, u32[]{:S(2)}, u32[]{:S(2)}) collective-permute-start(f32[768,128]{1,0:T(8,128)S(1)} %get-tuple-element.33), channel_id=1, source_target_pairs={{4,0},{8,4},{12,8},{16,12},{20,16},{24,20},{28,24},{0,28},{5,1},{9... | collective-permute-start | bytes 1179656 | tf_op jit(solution)/shard_map/ppermute | solution.py:16
  60.6 163.5 %collective-permute-start.9 = (s32[9]{0:T(128)S(1)}, s32[9]{0:T(128)S(1)}, u32[]{:S(2)}, u32[]{:S(2)}) collective-permute-start(s32[9]{0:T(128)S(1)} %get-tuple-element.50), channel_id=1, source_target_pairs={{4,0},{8,4},{12,8},{16,12},{20,16},{24,20},{28,24},{0,28},{5,1},{9... | collective-permute-start | bytes 116 | tf_op jit(solution)/shard_map/ppermute | solution.py:16
  60.6 168.0 %collective-permute-start.8 = (s32[9]{0:T(128)S(1)}, s32[9]{0:T(128)S(1)}, u32[]{:S(2)}, u32[]{:S(2)}) collective-permute-start(s32[9]{0:T(128)S(1)} %get-tuple-element.49), channel_id=1, source_target_pairs={{28,0},{0,4},{4,8},{8,12},{12,16},{16,20},{20,24},{24,28},{29,1},{... | collective-permute-start | bytes 116 | tf_op jit(solution)/shard_map/ppermute | solution.py:16
  63.2 249.4 %collective-permute-start.7 = (f32[8,16,16]{2,1,0:T(8,128)}, f32[8,16,16]{2,1,0:T(8,128)S(1)}, u32[]{:S(2)}, u32[]{:S(2)}) collective-permute-start(f32[8,16,16]{2,1,0:T(8,128)} %get-tuple-element.46), channel_id=1, source_target_pairs={{4,0},{8,4},{12,8},{16,12},{20,16},{24,20},{28,24},{0,28},{5,1},{9... | collective-permute-start | bytes 24584 | tf_op jit(solution)/shard_map/ppermute | solution.py:16
  66.0 246.7 %collective-permute-start.6 = (f32[8,16,16]{2,1,0:T(8,128)}, f32[8,16,16]{2,1,0:T(8,128)S(1)}, u32[]{:S(2)}, u32[]{:S(2)}) collective-permute-start(f32[8,16,16]{2,1,0:T(8,128)} %get-tuple-element.45), channel_id=1, source_target_pairs={{28,0},{0,4},{4,8},{8,12},{12,16},{16,20},{20,24},{24,28},{29,1},{... | collective-permute-start | bytes 24584 | tf_op jit(solution)/shard_map/ppermute | solution.py:16
  223.5 10.6 %collective-permute-start.2 = (f32[768,128]{1,0:T(8,128)S(1)}, f32[768,128]{1,0:T(8,128)S(1)}, u32[]{:S(2)}, u32[]{:S(2)}) collective-permute-start(f32[768,128]{1,0:T(8,128)S(1)} %get-tuple-element.41), channel_id=1, source_target_pairs={{28,0},{0,4},{4,8},{8,12},{12,16},{16,20},{20,24},{24,28},{29,1},{... | collective-permute-start | bytes 1179656 | tf_op jit(solution)/shard_map/ppermute | solution.py:16
  224.0 89.3 %collective-permute-start.5 = (bf16[16,1536]{1,0:T(8,128)(2,1)S(1)}, bf16[16,1536]{1,0:T(8,128)(2,1)S(1)}, u32[]{:S(2)}, u32[]{:S(2)}) collective-permute-start(bf16[16,1536]{1,0:T(8,128)(2,1)S(1)} %get-tuple-element.48), channel_id=1, source_target_pairs={{4,0},{8,4},{12,8},{16,12},{20,16},{24,20},{28,24},{0,28},{5,1},{9... | collective-permute-start | bytes 147464 | tf_op jit(solution)/shard_map/ppermute | solution.py:16
  234.1 83.4 %slice-start = ((s8[18874368]{0:T(1024)(128)(4,1)}), s8[4194304]{0:T(1024)(128)(4,1)S(1)}, s32[]{:S(2)}) async-start(s8[18874368]{0:T(1024)(128)(4,1)} %bitcast.148), calls=%async_computation | async-start | bytes 8388608
  234.1 83.4 %slice-start.1 = ((s8[18874368]{0:T(1024)(128)(4,1)}), s8[4194304]{0:T(1024)(128)(4,1)S(1)}, s32[]{:S(2)}) async-start(s8[18874368]{0:T(1024)(128)(4,1)} %bitcast.148), calls=%async_computation.1 | async-start | bytes 8388608
  234.1 83.4 %slice-start.2 = ((s8[18874368]{0:T(1024)(128)(4,1)}), s8[4194304]{0:T(1024)(128)(4,1)S(1)}, s32[]{:S(2)}) async-start(s8[18874368]{0:T(1024)(128)(4,1)} %bitcast.148), calls=%async_computation.2 | async-start | bytes 8388608
  267.1 8.4 %collective-permute-start.3 = (f32[768,128]{1,0:T(8,128)S(1)}, f32[768,128]{1,0:T(8,128)S(1)}, u32[]{:S(2)}, u32[]{:S(2)}) collective-permute-start(f32[768,128]{1,0:T(8,128)S(1)} %get-tuple-element.30), channel_id=1, source_target_pairs={{4,0},{8,4},{12,8},{16,12},{20,16},{24,20},{28,24},{0,28},{5,1},{9... | collective-permute-start | bytes 1179656 | tf_op jit(solution)/shard_map/ppermute | solution.py:16
  269.9 10.6 %collective-permute-start.10 = (f32[768,128]{1,0:T(8,128)S(1)}, f32[768,128]{1,0:T(8,128)S(1)}, u32[]{:S(2)}, u32[]{:S(2)}) collective-permute-start(f32[768,128]{1,0:T(8,128)S(1)} %get-tuple-element.29), channel_id=1, source_target_pairs={{28,0},{0,4},{4,8},{8,12},{12,16},{16,20},{20,24},{24,28},{29,1},{... | collective-permute-start | bytes 1179656 | tf_op jit(solution)/shard_map/ppermute | solution.py:16
  275.5 37.8 %collective-permute-start.4 = (bf16[16,1536]{1,0:T(8,128)(2,1)S(1)}, bf16[16,1536]{1,0:T(8,128)(2,1)S(1)}, u32[]{:S(2)}, u32[]{:S(2)}) collective-permute-start(bf16[16,1536]{1,0:T(8,128)(2,1)S(1)} %get-tuple-element.47), channel_id=1, source_target_pairs={{28,0},{0,4},{4,8},{8,12},{12,16},{16,20},{20,24},{24,28},{29,1},{... | collective-permute-start | bytes 147464 | tf_op jit(solution)/shard_map/ppermute | solution.py:16
  280.8 36.7 %slice-start.3 = ((s8[18874368]{0:T(1024)(128)(4,1)}), s8[4194304]{0:T(1024)(128)(4,1)S(1)}, s32[]{:S(2)}) async-start(s8[18874368]{0:T(1024)(128)(4,1)} %bitcast.148), calls=%async_computation.3 | async-start | bytes 8388608
  349.3 7.9 %collective-permute-start.11 = (f32[768,128]{1,0:T(8,128)S(1)}, f32[768,128]{1,0:T(8,128)S(1)}, u32[]{:S(2)}, u32[]{:S(2)}) collective-permute-start(f32[768,128]{1,0:T(8,128)S(1)} %get-tuple-element.27), channel_id=1, source_target_pairs={{4,0},{8,4},{12,8},{16,12},{20,16},{24,20},{28,24},{0,28},{5,1},{9... | collective-permute-start | bytes 1179656 | tf_op jit(solution)/shard_map/ppermute | solution.py:16
  350.9 10.6 %collective-permute-start.12 = (f32[768,128]{1,0:T(8,128)S(1)}, f32[768,128]{1,0:T(8,128)S(1)}, u32[]{:S(2)}, u32[]{:S(2)}) collective-permute-start(f32[768,128]{1,0:T(8,128)S(1)} %get-tuple-element.26), channel_id=1, source_target_pairs={{28,0},{0,4},{4,8},{8,12},{12,16},{16,20},{20,24},{24,28},{29,1},{... | collective-permute-start | bytes 1179656 | tf_op jit(solution)/shard_map/ppermute | solution.py:16
  432.8 9.4 %copy-start.1 = (f32[2,1536,128]{2,1,0:T(8,128)S(1)}, f32[2,1536,128]{2,1,0:T(8,128)}, u32[]{:S(2)}) copy-start(f32[2,1536,128]{2,1,0:T(8,128)} %fusion.20) | copy-start | bytes 4718596
  434.3 7.9 %collective-permute-start.13 = (f32[768,128]{1,0:T(8,128)S(1)}, f32[768,128]{1,0:T(8,128)S(1)}, u32[]{:S(2)}, u32[]{:S(2)}) collective-permute-start(f32[768,128]{1,0:T(8,128)S(1)} %get-tuple-element.24), channel_id=1, source_target_pairs={{4,0},{8,4},{12,8},{16,12},{20,16},{24,20},{28,24},{0,28},{5,1},{9... | collective-permute-start | bytes 1179656 | tf_op jit(solution)/shard_map/ppermute | solution.py:16
  436.3 10.6 %collective-permute-start.14 = (f32[768,128]{1,0:T(8,128)S(1)}, f32[768,128]{1,0:T(8,128)S(1)}, u32[]{:S(2)}, u32[]{:S(2)}) collective-permute-start(f32[768,128]{1,0:T(8,128)S(1)} %get-tuple-element.23), channel_id=1, source_target_pairs={{28,0},{0,4},{4,8},{8,12},{12,16},{16,20},{20,24},{24,28},{29,1},{... | collective-permute-start | bytes 1179656 | tf_op jit(solution)/shard_map/ppermute | solution.py:16
  447.2 32.4 %copy-start.7 = (f32[2,768,128]{2,1,0:T(8,128)}, f32[2,768,128]{2,1,0:T(8,128)S(1)}, u32[]{:S(2)}) copy-start(f32[2,768,128]{2,1,0:T(8,128)S(1)} %maximum_negate_fusion.4) | copy-start | bytes 2359300
  516.7 7.9 %collective-permute-start.15 = (f32[768,128]{1,0:T(8,128)S(1)}, f32[768,128]{1,0:T(8,128)S(1)}, u32[]{:S(2)}, u32[]{:S(2)}) collective-permute-start(f32[768,128]{1,0:T(8,128)S(1)} %get-tuple-element.21), channel_id=1, source_target_pairs={{4,0},{8,4},{12,8},{16,12},{20,16},{24,20},{28,24},{0,28},{5,1},{9... | collective-permute-start | bytes 1179656 | tf_op jit(solution)/shard_map/ppermute | solution.py:16
  518.5 10.5 %collective-permute-start.16 = (f32[768,128]{1,0:T(8,128)S(1)}, f32[768,128]{1,0:T(8,128)S(1)}, u32[]{:S(2)}, u32[]{:S(2)}) collective-permute-start(f32[768,128]{1,0:T(8,128)S(1)} %get-tuple-element.20), channel_id=1, source_target_pairs={{28,0},{0,4},{4,8},{8,12},{12,16},{16,20},{20,24},{24,28},{29,1},{... | collective-permute-start | bytes 1179656 | tf_op jit(solution)/shard_map/ppermute | solution.py:16
  (13 other events, 29.9 us)
where the time goes:
time: 601 us; the launch traced here: 592 us
  local copies, waits for them, and re-layouts  181 us (30%)
  blocking collectives  178 us (30%)
  matrix products  146 us (24%)
  waiting for transfers between devices  45.1 us (8%)
  starting transfers between devices  24.3 us (4%)
  other arithmetic  16.3 us (3%)
    gather x3, local copies, waits for them, and re-layouts, shards(): matrix[ordering].T[ordering]  155 us
    all_gather x5, blocking collectives, gather_coefficients(): return lax.all_gather(coefficients, 'dom', axis=0, tiled=True)  153 us
    dot_general x4, matrix products, shards(): jnp.einsum('smn,smc->snc', slot_ops, local_direction, precision=highest)  130 us
    ppermute x17, waiting for transfers between devices, from_behind(): return lax.ppermute(block, axis, route)  45.1 us
    ppermute x17, starting transfers between devices, from_behind(): return lax.ppermute(block, axis, route)  24.3 us
    psum x1, blocking collectives, shards(): norm_list.append(jnp.sqrt(lax.psum(partial_value, 'dom') + epsilon))  19.1 us
    gather x3, local copies, waits for them, and re-layouts, shards(): block_rows[:, ordering]  16.7 us
  transfers between devices with their start and end apart: 17, of which 9 were waited for; matrix products, arithmetic and copies ran while one was open for 36% of the time, Pallas kernels for 0%

commit v1 on v0

--- a/solution.py
+++ b/solution.py
@@ -8,6 +8,19 @@
 high_bound = 14.0
 epsilon = 1e-06
 highest = lax.Precision.HIGHEST
+
+
+def gather_around(value, axis, dim):
+    ways = lax.axis_size(axis)
+    up = [(d, (d + 1) % ways) for d in range(ways)]
+    down = [(d, (d - 1) % ways) for d in range(ways)]
+    earlier, later = ([value], [value])
+    for _ in range(ways // 2):
+        earlier.append(lax.ppermute(earlier[-1], axis, up))
+    for _ in range((ways - 1) // 2):
+        later.append(lax.ppermute(later[-1], axis, down))
+    line = jnp.concatenate([*earlier[::-1], *later[1:]], axis=dim)
+    return jnp.roll(line, (lax.axis_index(axis) - ways // 2) * value.shape[dim], axis=dim)
 
 
 def from_behind(block, axis, distance):
@@ -65,7 +78,7 @@
         coefficients = jnp.einsum("sjn,snc->sjc", slot_modes, slot_rows, precision=highest).astype(
             jnp.bfloat16
         )
-        return lax.all_gather(coefficients, "dom", axis=0, tiled=True)
+        return gather_around(coefficients, "dom", 0)
 
     centre = 0.5 * (high_bound + low_bound)
     radius = 0.5 * (high_bound - low_bound)

time: 601 us -> 598 us (level)
  blocking collectives: 178 us -> 28 us
  starting transfers between devices: 24.3 us -> 112 us
  waiting for transfers between devices: 45.1 us -> 98.3 us
    all_gather x5 -> x0, blocking collectives: 153 us -> none  [gather_coefficients(): return lax.all_gather(coefficients, 'dom', axis=0, tiled=True)]
    ppermute x0 -> x35, starting transfers between devices: none -> 71 us  [the longest x15 69.2 us: gather_around(): later.append(lax.ppermute(later[-1], axis, down))]
    ppermute x0 -> x35, waiting for transfers between devices: none -> 53.3 us  [the longest x20 53.3 us: gather_around(): earlier.append(lax.ppermute(earlier[-1], axis, up))]
    ppermute x17, starting transfers between devices: 24.3 us -> 41 us  [from_behind(): return lax.ppermute(block, axis, route)]
  transfers between devices with their start and end apart: 17 -> 52, of which waited for: 9 -> 28; matrix products, arithmetic and copies ran while one was open for 36% -> 30% of each run, Pallas kernels for 0% -> 0%
where the time goes in v1:
time: 598 us; the launch traced here: 589 us
  local copies, waits for them, and re-layouts  185 us (31%)
  matrix products  148 us (25%)
  starting transfers between devices  112 us (19%)
  waiting for transfers between devices  98.3 us (16%)
  blocking collectives  28 us (5%)
  other arithmetic  16.1 us (3%)
    gather x3, local copies, waits for them, and re-layouts, shards(): matrix[ordering].T[ordering]  155 us
    dot_general x4, matrix products, shards(): jnp.einsum('smn,smc->snc', slot_ops, local_direction, precision=highest)  132 us
    ppermute x15, starting transfers between devices, gather_around(): later.append(lax.ppermute(later[-1], axis, down))  69.2 us
    ppermute x20, waiting for transfers between devices, gather_around(): earlier.append(lax.ppermute(earlier[-1], axis, up))  53.3 us
    ppermute x17, waiting for transfers between devices, from_behind(): return lax.ppermute(block, axis, route)  45 us
    ppermute x17, starting transfers between devices, from_behind(): return lax.ppermute(block, axis, route)  41 us
    psum x1, blocking collectives, shards(): norm_list.append(jnp.sqrt(lax.psum(partial_value, 'dom') + epsilon))  21.8 us
    gather x3, local copies, waits for them, and re-layouts, shards(): block_rows[:, ordering]  16.7 us
  transfers between devices with their start and end apart: 52, of which 28 were waited for; matrix products, arithmetic and copies ran while one was open for 30% of the time, Pallas kernels for 0%

profile of v1, /device:TPU:0, one launch (start us, length us, event | category | flops | bytes accessed | tf_op | source)
XLA Modules:
  0.0 589.0 jit_solution(4666028566387051927)
XLA Ops:
  7.0 16.5 %gather_fusion = bf16[3072,16]{1,0:T(8,128)(2,1)S(1)} fusion(bf16[2,16,1536]{1,2,0:T(8,128)(2,1)S(1)} %copy.18, s32[3072]{0:T(1024)S(1)} %reshape.35), kind=kCustom, calls=%fused_computation | custom fusion | bytes 221184 | tf_op jit(solution)/shard_map/vmap()/gather | solution.py:43
  26.1 4.8 collective-permute-done.1
  57.3 5.2 collective-permute-done.8
  65.1 5.3 collective-permute-start.16
  70.4 68.1 %gather_fusion.1 = f32[3072,1536]{1,0:T(8,128)} fusion(f32[2,1536,1536]{2,1,0:T(8,128)} %param.9, s32[3072]{0:T(1024)S(1)} %reshape.35), kind=kCustom, calls=%fused_computation.1 | custom fusion | bytes 37773312 | tf_op jit(solution)/shard_map/vmap()/gather | solution.py:42
  138.4 18.7 %copy.22 = f32[2,1536,1536]{1,2,0:T(8,128)} copy(f32[2,1536,1536]{2,1,0:T(8,128)} %bitcast.148) | data formatting | bytes 37748736 | tf_op jit(solution)/shard_map/vmap()/gather | solution.py:42
  157.1 68.1 %gather_fusion.2 = f32[3072,1536]{1,0:T(8,128)} fusion(f32[2,1536,1536]{2,1,0:T(8,128)} %bitcast.141, s32[3072]{0:T(1024)S(1)} %reshape.35), kind=kCustom, calls=%fused_computation.2 | custom fusion | bytes 37773312 | tf_op jit(solution)/shard_map/vmap()/gather | solution.py:42
  225.4 33.0 %fusion.18 = f32[2,1536,128]{2,1,0:T(8,128)S(1)} fusion(f32[2,1536,1536]{2,1,0:T(8,128)} %bitcast.142, f32[2,768,128]{2,1,0:T(8,128)S(1)} %fusion.44, f32[2,768,128]{2,1,0:T(8,128)S(1)} %maximum_negate_fusion.1), kind=kOutput, calls=%fused_computation.29 | convolution fusion | flops 7248543744 | bytes 22020096 | tf_op jit(solution)/shard_map/smn,smc->snc/dot_general | solution.py:103
  258.5 4.8 collective-permute-start.10
  263.7 6.2 %collective-permute-done.10 = f32[768,128]{1,0:T(8,128)S(1)} collective-permute-done((f32[768,128]{1,0:T(8,128)S(1)}, f32[768,128]{1,0:T(8,128)S(1)}, u32[]{:S(2)}, u32[]{:S(2)}) %collective-permute-start.10) | collective-permute-done | bytes 393248 | tf_op jit(solution)/shard_map/ppermute | solution.py:29
  275.4 6.4 %collective-permute-done.18 = bf16[2,16,128]{2,1,0:T(8,128)(2,1)S(1)} collective-permute-done((bf16[2,16,128]{2,1,0:T(8,128)(2,1)S(1)}, bf16[2,16,128]{2,1,0:T(8,128)(2,1)S(1)}, u32[]{:S(2)}, u32[]{:S(2)}) %collective-permute-start.18) | collective-permute-done | bytes 8224 | tf_op jit(solution)/shard_map/ppermute | solution.py:19
  316.7 33.4 %fusion.120 = f32[2,1536,128]{2,1,0:T(8,128)S(1)} fusion(f32[2,1536,1536]{2,1,0:T(8,128)} %bitcast.143, f32[2,1536,128]{2,1,0:T(8,128)S(1)} %multiply_add_fusion.1), kind=kOutput, calls=%fused_computation.240 | convolution fusion | flops 7247757312 | bytes 22020096 | tf_op jit(solution)/shard_map/smn,smc->snc/dot_general | solution.py:103
  354.4 5.3 collective-permute-done.25
  360.1 4.9 collective-permute-done.26
  366.3 6.4 %collective-permute-done.27 = bf16[2,16,128]{2,1,0:T(8,128)(2,1)S(1)} collective-permute-done((bf16[2,16,128]{2,1,0:T(8,128)(2,1)S(1)}, bf16[2,16,128]{2,1,0:T(8,128)(2,1)S(1)}, u32[]{:S(2)}, u32[]{:S(2)}) %collective-permute-start.27) | collective-permute-done | bytes 8224 | tf_op jit(solution)/shard_map/ppermute | solution.py:19
  397.7 33.2 %fusion.20 = f32[2,1536,128]{2,1,0:T(8,128)} fusion(f32[2,1536,1536]{2,1,0:T(8,128)S(1)} %bitcast.146, f32[2,1536,128]{2,1,0:T(8,128)} %fusion.5, f32[2,1536,128]{2,1,0:T(8,128)S(1)} %multiply_add_fusion.1), kind=kOutput, calls=%fused_computation.31 | convolution fusion | flops 7248936960 | bytes 23592960 | tf_op jit(solution)/shard_map/smn,smc->snc/dot_general | solution.py:103
  437.0 5.3 collective-permute-done.34
  442.7 5.0 collective-permute-done.35
  448.9 6.3 %collective-permute-done.36 = bf16[2,16,128]{2,1,0:T(8,128)(2,1)S(1)} collective-permute-done((bf16[2,16,128]{2,1,0:T(8,128)(2,1)S(1)}, bf16[2,16,128]{2,1,0:T(8,128)(2,1)S(1)}, u32[]{:S(2)}, u32[]{:S(2)}) %collective-permute-start.36) | collective-permute-done | bytes 8224 | tf_op jit(solution)/shard_map/ppermute | solution.py:19
  480.0 32.5 %fusion.9 = f32[2,1536,128]{2,1,0:T(8,128)S(1)} fusion(f32[2,1536,1536]{2,1,0:T(8,128)S(1)} %bitcast.147, f32[2,1536,128]{2,1,0:T(8,128)S(1)} %copy-done.2, f32[2,768,128]{2,1,0:T(8,128)} %get-tuple-element.36, f32[2,768,128]{2,1,0:T(8,128)} %get-tuple-element.35, f32[2,1536,128]{2,1,0:T(8,128)S(1)} %multiply_add_fusion.1, f32[2,768,128]{2,1,0:T(8,128)S(1)} %fusion.40, ...), kind=kOutput, calls=%fused_computation.19 | convolution fusion | flops 7251689472 | bytes 26738688 | tf_op jit(solution)/shard_map/smn,smc->snc/dot_general | solution.py:103
  517.3 5.4 collective-permute-done.43
  529.0 6.3 %collective-permute-done.45 = bf16[2,16,128]{2,1,0:T(8,128)(2,1)S(1)} collective-permute-done((bf16[2,16,128]{2,1,0:T(8,128)(2,1)S(1)}, bf16[2,16,128]{2,1,0:T(8,128)(2,1)S(1)}, u32[]{:S(2)}, u32[]{:S(2)}) %collective-permute-start.45) | collective-permute-done | bytes 8224 | tf_op jit(solution)/shard_map/ppermute | solution.py:19
  560.1 21.8 %all-reduce = (f32[128]{0:T(128)S(1)}, f32[128]{0:T(128)S(1)}, f32[128]{0:T(128)S(1)}, f32[128]{0:T(128)S(1)}) all-reduce(f32[128]{0:T(128)S(1)} %get-tuple-element.17, f32[128]{0:T(128)S(1)} %get-tuple-element.15, f32[128]{0:T(128)S(1)} %get-tuple-element.13, f32[128]{0:T(128)S(1)} %get-tuple-element.11), channel_id=1, replica_groups=mesh['dom'=8,'case'=4] {'dom'}, use_global_device_ids=true, to_apply=%region_7.9 | all-reduce | flops 512 | bytes 4096 | tf_op jit(solution)/shard_map/psum | solution.py:124
  582.7 6.2 %pmax.7 = f32[4]{0:T(128)} all-reduce(f32[4]{0:T(128)S(1)} %get-tuple-element.9), channel_id=1, replica_groups=mesh['dom'=8,'case'=4] {'case'}, use_global_device_ids=true, to_apply=%region_9.11 | all-reduce | flops 4 | bytes 32 | tf_op jit(solution)/shard_map/pmax | solution.py:134
  (272 shorter events, 178.3 us)
Async XLA Ops:
  3.6 19.9 %collective-permute-start = (f32[768,128]{1,0:T(8,128)}, f32[768,128]{1,0:T(8,128)S(1)}, u32[]{:S(2)}, u32[]{:S(2)}) collective-permute-start(f32[768,128]{1,0:T(8,128)} %get-tuple-element.44), channel_id=1, source_target_pairs={{28,0},{0,4},{4,8},{8,12},{12,16},{16,20},{20,24},{24,28},{29,1},{... | collective-permute-start | bytes 1179656 | tf_op jit(solution)/shard_map/ppermute | solution.py:29
  37.3 6.5 %collective-permute-start.6 = (bf16[2,16,128]{2,1,0:T(8,128)(2,1)S(1)}, bf16[2,16,128]{2,1,0:T(8,128)(2,1)S(1)}, u32[]{:S(2)}, u32[]{:S(2)}) collective-permute-start(bf16[2,16,128]{2,1,0:T(8,128)(2,1)S(1)} %collective-permute-done.5), channel_id=1, source_target_pairs={{0,28},{4,0},{8,4},{12,8},{16,12},{20,16},{24,20},{28,24},{1,29},{... | collective-permute-start | bytes 24584 | tf_op jit(solution)/shard_map/ppermute | solution.py:21
  52.5 10.0 %collective-permute-start.8 = (f32[768,128]{1,0:T(8,128)S(1)}, f32[768,128]{1,0:T(8,128)S(1)}, u32[]{:S(2)}, u32[]{:S(2)}) collective-permute-start(f32[768,128]{1,0:T(8,128)S(1)} %get-tuple-element.34), channel_id=1, source_target_pairs={{4,0},{8,4},{12,8},{16,12},{20,16},{24,20},{28,24},{0,28},{5,1},{9... | collective-permute-start | bytes 1179656 | tf_op jit(solution)/shard_map/ppermute | solution.py:29
  64.9 160.3 %collective-permute-start.9 = (f32[768,128]{1,0:T(8,128)S(1)}, f32[768,128]{1,0:T(8,128)S(1)}, u32[]{:S(2)}, u32[]{:S(2)}) collective-permute-start(f32[768,128]{1,0:T(8,128)S(1)} %get-tuple-element.42), channel_id=1, source_target_pairs={{28,0},{0,4},{4,8},{8,12},{12,16},{16,20},{20,24},{24,28},{29,1},{... | collective-permute-start | bytes 1179656 | tf_op jit(solution)/shard_map/ppermute | solution.py:29
  65.1 160.1 %collective-permute-start.16 = (s32[9]{0:T(128)S(1)}, s32[9]{0:T(128)S(1)}, u32[]{:S(2)}, u32[]{:S(2)}) collective-permute-start(s32[9]{0:T(128)S(1)} %get-tuple-element.51), channel_id=1, source_target_pairs={{4,0},{8,4},{12,8},{16,12},{20,16},{24,20},{28,24},{0,28},{5,1},{9... | collective-permute-start | bytes 116 | tf_op jit(solution)/shard_map/ppermute | solution.py:29
  70.4 154.8 %collective-permute-start.15 = (s32[9]{0:T(128)S(1)}, s32[9]{0:T(128)S(1)}, u32[]{:S(2)}, u32[]{:S(2)}) collective-permute-start(s32[9]{0:T(128)S(1)} %get-tuple-element.50), channel_id=1, source_target_pairs={{28,0},{0,4},{4,8},{8,12},{12,16},{16,20},{20,24},{24,28},{29,1},{... | collective-permute-start | bytes 116 | tf_op jit(solution)/shard_map/ppermute | solution.py:29
  258.5 11.3 %collective-permute-start.10 = (f32[768,128]{1,0:T(8,128)S(1)}, f32[768,128]{1,0:T(8,128)S(1)}, u32[]{:S(2)}, u32[]{:S(2)}) collective-permute-start(f32[768,128]{1,0:T(8,128)S(1)} %get-tuple-element.31), channel_id=1, source_target_pairs={{4,0},{8,4},{12,8},{16,12},{20,16},{24,20},{28,24},{0,28},{5,1},{9... | collective-permute-start | bytes 1179656 | tf_op jit(solution)/shard_map/ppermute | solution.py:29
  263.5 10.6 %collective-permute-start.17 = (f32[768,128]{1,0:T(8,128)S(1)}, f32[768,128]{1,0:T(8,128)S(1)}, u32[]{:S(2)}, u32[]{:S(2)}) collective-permute-start(f32[768,128]{1,0:T(8,128)S(1)} %get-tuple-element.30), channel_id=1, source_target_pairs={{28,0},{0,4},{4,8},{8,12},{12,16},{16,20},{20,24},{24,28},{29,1},{... | collective-permute-start | bytes 1179656 | tf_op jit(solution)/shard_map/ppermute | solution.py:29
  275.4 6.5 %collective-permute-start.18 = (bf16[2,16,128]{2,1,0:T(8,128)(2,1)S(1)}, bf16[2,16,128]{2,1,0:T(8,128)(2,1)S(1)}, u32[]{:S(2)}, u32[]{:S(2)}) collective-permute-start(bf16[2,16,128]{2,1,0:T(8,128)(2,1)S(1)} %fusion.27), channel_id=1, source_target_pairs={{0,4},{4,8},{8,12},{12,16},{16,20},{20,24},{24,28},{28,0},{1,5},{5... | collective-permute-start | bytes 24584 | tf_op jit(solution)/shard_map/ppermute | solution.py:19
  281.9 6.5 %collective-permute-start.19 = (bf16[2,16,128]{2,1,0:T(8,128)(2,1)S(1)}, bf16[2,16,128]{2,1,0:T(8,128)(2,1)}, u32[]{:S(2)}, u32[]{:S(2)}) collective-permute-start(bf16[2,16,128]{2,1,0:T(8,128)(2,1)S(1)} %collective-permute-done.18), channel_id=1, source_target_pairs={{0,4},{4,8},{8,12},{12,16},{16,20},{20,24},{24,28},{28,0},{1,5},{5... | collective-permute-start | bytes 24584 | tf_op jit(solution)/shard_map/ppermute | solution.py:19
  281.9 12.2 %collective-permute-start.22 = (bf16[2,16,128]{2,1,0:T(8,128)(2,1)S(1)}, bf16[2,16,128]{2,1,0:T(8,128)(2,1)}, u32[]{:S(2)}, u32[]{:S(2)}) collective-permute-start(bf16[2,16,128]{2,1,0:T(8,128)(2,1)S(1)} %fusion.27), channel_id=1, source_target_pairs={{0,28},{4,0},{8,4},{12,8},{16,12},{20,16},{24,20},{28,24},{1,29},{... | collective-permute-start | bytes 24584 | tf_op jit(solution)/shard_map/ppermute | solution.py:21
  288.4 10.4 %collective-permute-start.20 = (bf16[2,16,128]{2,1,0:T(8,128)(2,1)}, bf16[2,16,128]{2,1,0:T(8,128)(2,1)}, u32[]{:S(2)}, u32[]{:S(2)}) collective-permute-start(bf16[2,16,128]{2,1,0:T(8,128)(2,1)} %collective-permute-done.19), channel_id=1, source_target_pairs={{0,4},{4,8},{8,12},{12,16},{16,20},{20,24},{24,28},{28,0},{1,5},{5... | collective-permute-start | bytes 24584 | tf_op jit(solution)/shard_map/ppermute | solution.py:19
  289.1 21.8 %collective-permute-start.14 = (f32[8,16,16]{2,1,0:T(8,128)}, f32[8,16,16]{2,1,0:T(8,128)S(1)}, u32[]{:S(2)}, u32[]{:S(2)}) collective-permute-start(f32[8,16,16]{2,1,0:T(8,128)} %get-tuple-element.47), channel_id=1, source_target_pairs={{4,0},{8,4},{12,8},{16,12},{20,16},{24,20},{28,24},{0,28},{5,1},{9... | collective-permute-start | bytes 24584 | tf_op jit(solution)/shard_map/ppermute | solution.py:29
  293.8 17.1 %collective-permute-start.13 = (f32[8,16,16]{2,1,0:T(8,128)}, f32[8,16,16]{2,1,0:T(8,128)S(1)}, u32[]{:S(2)}, u32[]{:S(2)}) collective-permute-start(f32[8,16,16]{2,1,0:T(8,128)} %get-tuple-element.46), channel_id=1, source_target_pairs={{28,0},{0,4},{4,8},{8,12},{12,16},{16,20},{20,24},{24,28},{29,1},{... | collective-permute-start | bytes 24584 | tf_op jit(solution)/shard_map/ppermute | solution.py:29
  294.0 9.6 %collective-permute-start.23 = (bf16[2,16,128]{2,1,0:T(8,128)(2,1)}, bf16[2,16,128]{2,1,0:T(8,128)(2,1)S(1)}, u32[]{:S(2)}, u32[]{:S(2)}) collective-permute-start(bf16[2,16,128]{2,1,0:T(8,128)(2,1)} %collective-permute-done.22), channel_id=1, source_target_pairs={{0,28},{4,0},{8,4},{12,8},{16,12},{20,16},{24,20},{28,24},{1,29},{... | collective-permute-start | bytes 24584 | tf_op jit(solution)/shard_map/ppermute | solution.py:21
  298.8 6.6 %collective-permute-start.21 = (bf16[2,16,128]{2,1,0:T(8,128)(2,1)}, bf16[2,16,128]{2,1,0:T(8,128)(2,1)S(1)}, u32[]{:S(2)}, u32[]{:S(2)}) collective-permute-start(bf16[2,16,128]{2,1,0:T(8,128)(2,1)} %collective-permute-done.20), channel_id=1, source_target_pairs={{0,4},{4,8},{8,12},{12,16},{16,20},{20,24},{24,28},{28,0},{1,5},{5... | collective-permute-start | bytes 24584 | tf_op jit(solution)/shard_map/ppermute | solution.py:19
  298.8 12.7 %collective-permute-start.12 = (bf16[16,1536]{1,0:T(8,128)(2,1)S(1)}, bf16[16,1536]{1,0:T(8,128)(2,1)S(1)}, u32[]{:S(2)}, u32[]{:S(2)}) collective-permute-start(bf16[16,1536]{1,0:T(8,128)(2,1)S(1)} %get-tuple-element.49), channel_id=1, source_target_pairs={{4,0},{8,4},{12,8},{16,12},{20,16},{24,20},{28,24},{0,28},{5,1},{9... | collective-permute-start | bytes 147464 | tf_op jit(solution)/shard_map/ppermute | solution.py:29
  303.6 7.9 %collective-permute-start.11 = (bf16[16,1536]{1,0:T(8,128)(2,1)S(1)}, bf16[16,1536]{1,0:T(8,128)(2,1)S(1)}, u32[]{:S(2)}, u32[]{:S(2)}) collective-permute-start(bf16[16,1536]{1,0:T(8,128)(2,1)S(1)} %get-tuple-element.48), channel_id=1, source_target_pairs={{28,0},{0,4},{4,8},{8,12},{12,16},{16,20},{20,24},{24,28},{29,1},{... | collective-permute-start | bytes 147464 | tf_op jit(solution)/shard_map/ppermute | solution.py:29
  350.2 9.5 %collective-permute-start.25 = (f32[768,128]{1,0:T(8,128)S(1)}, f32[768,128]{1,0:T(8,128)S(1)}, u32[]{:S(2)}, u32[]{:S(2)}) collective-permute-start(f32[768,128]{1,0:T(8,128)S(1)} %get-tuple-element.28), channel_id=1, source_target_pairs={{4,0},{8,4},{12,8},{16,12},{20,16},{24,20},{28,24},{0,28},{5,1},{9... | collective-permute-start | bytes 1179656 | tf_op jit(solution)/shard_map/ppermute | solution.py:29
  354.4 10.6 %collective-permute-start.26 = (f32[768,128]{1,0:T(8,128)S(1)}, f32[768,128]{1,0:T(8,128)S(1)}, u32[]{:S(2)}, u32[]{:S(2)}) collective-permute-start(f32[768,128]{1,0:T(8,128)S(1)} %get-tuple-element.27), channel_id=1, source_target_pairs={{28,0},{0,4},{4,8},{8,12},{12,16},{16,20},{20,24},{24,28},{29,1},{... | collective-permute-start | bytes 1179656 | tf_op jit(solution)/shard_map/ppermute | solution.py:29
  432.3 10.0 %collective-permute-start.34 = (f32[768,128]{1,0:T(8,128)S(1)}, f32[768,128]{1,0:T(8,128)S(1)}, u32[]{:S(2)}, u32[]{:S(2)}) collective-permute-start(f32[768,128]{1,0:T(8,128)S(1)} %get-tuple-element.25), channel_id=1, source_target_pairs={{4,0},{8,4},{12,8},{16,12},{20,16},{24,20},{28,24},{0,28},{5,1},{9... | collective-permute-start | bytes 1179656 | tf_op jit(solution)/shard_map/ppermute | solution.py:29
  437.0 10.6 %collective-permute-start.35 = (f32[768,128]{1,0:T(8,128)S(1)}, f32[768,128]{1,0:T(8,128)S(1)}, u32[]{:S(2)}, u32[]{:S(2)}) collective-permute-start(f32[768,128]{1,0:T(8,128)S(1)} %get-tuple-element.24), channel_id=1, source_target_pairs={{28,0},{0,4},{4,8},{8,12},{12,16},{16,20},{20,24},{24,28},{29,1},{... | collective-permute-start | bytes 1179656 | tf_op jit(solution)/shard_map/ppermute | solution.py:29
  512.6 10.1 %collective-permute-start.43 = (f32[768,128]{1,0:T(8,128)S(1)}, f32[768,128]{1,0:T(8,128)S(1)}, u32[]{:S(2)}, u32[]{:S(2)}) collective-permute-start(f32[768,128]{1,0:T(8,128)S(1)} %get-tuple-element.22), channel_id=1, source_target_pairs={{4,0},{8,4},{12,8},{16,12},{20,16},{24,20},{28,24},{0,28},{5,1},{9... | collective-permute-start | bytes 1179656 | tf_op jit(solution)/shard_map/ppermute | solution.py:29
  517.3 10.5 %collective-permute-start.44 = (f32[768,128]{1,0:T(8,128)S(1)}, f32[768,128]{1,0:T(8,128)S(1)}, u32[]{:S(2)}, u32[]{:S(2)}) collective-permute-start(f32[768,128]{1,0:T(8,128)S(1)} %get-tuple-element.21), channel_id=1, source_target_pairs={{28,0},{0,4},{4,8},{8,12},{12,16},{16,20},{20,24},{24,28},{29,1},{... | collective-permute-start | bytes 1179656 | tf_op jit(solution)/shard_map/ppermute | solution.py:29
  (58 other events, 642.6 us)
